TPU v7x, 32 devices: a whole 2x2x4 slice. The times are simulated.
32 devices in a mesh: groups: 2 (over x), frames: 16 (over z, y, core).
Axes of the slice: x: 2, y: 2, z: 4, core: 2. Of those that a mesh axis runs over, the one named last changes fastest.
Arguments:
- video: float32 [4, 16, 256, 256], P('groups', 'frames'), parts along dimension 0, may hold values from -9 to 9
- clip_start: int32 [4], P('groups'), parts along dimension 0, may hold values from 0 to 7
- gain_space: float32 [256], replicated, may hold values from 0.1 to 1.9
- qkv_space: float32 [256, 768], replicated, may hold values from -0.375 to 0.375
- out_space: float32 [256, 256], replicated, may hold values from -0.375 to 0.375
- gain_time: float32 [256], replicated, may hold values from 0.1 to 1.9
- qkv_time: float32 [256, 768], replicated, may hold values from -0.375 to 0.375
- out_time: float32 [256, 256], replicated, may hold values from -0.375 to 0.375
- code_sums: float32 [8192, 256], P(('groups', 'frames')), parts along dimension 0, may hold values from -12 to 12
- code_counts: float32 [8192], P(('groups', 'frames')), parts along dimension 0, may hold values from 1 to 10
Outputs:
- latents: float32 [4, 16, 256, 256], P('groups', None, 'frames'), parts along dimension 0
- new_sums: float32 [8192, 256], P(('groups', 'frames')), parts along dimension 0
- new_counts: float32 [8192], P(('groups', 'frames')), parts along dimension 0
- new_codebook: float32 [8192, 256], P(('groups', 'frames')), parts along dimension 0
There are 2 independent parts, one for each index of `groups`. A program takes and returns all parts, laid end to end along the dimension named above; an argument that names none is the same for every part. Nothing has to cross between parts.
All inputs are finite; a program needn't handle non-finite values.
Results may differ from a plain program's by a relative error of at most 0.0003.
Values sent between devices are 32-bit elements; how exact they have to be, the bound alone decides.
A program may use at most 64 MiB of HBM per device.

v0:
```python
import functools

import jax
import jax.numpy as jnp
from jax import lax
from jax.experimental import pallas as pl
from jax.experimental.pallas import tpu as pltpu
from jax.sharding import PartitionSpec as P

HEADS = 4
ATTN_SCALE = 10.0
SOFTMAX_WARMTH = 0.05
DECAY_RATE = 0.9
EPSILON = 1e-06
F32 = jnp.float32
BF16 = jnp.bfloat16
NN = (((1,), (0,)), ((), ()))
NT = (((1,), (1,)), ((), ()))


def split(a):
    hi = a.astype(BF16)
    return hi, (a - hi.astype(F32)).astype(BF16)


def dot(a, b, dims=NN):
    return lax.dot_general(a, b, dims, preferred_element_type=F32)


def dot3(a, b, dims=NN):
    return dot(a[0], b[0], dims) + (dot(a[0], b[1], dims) + dot(a[1], b[0], dims))


def dot2(a, b, dims=NN):
    return dot(a[0], b, dims) + dot(a[1], b, dims)


def attention(x, gain, w_qkv, w_out, mask):
    rows, width = x.shape
    hd = width // HEADS
    lane_i = lax.broadcasted_iota(jnp.int32, (width, width), 0) // hd
    lane_j = lax.broadcasted_iota(jnp.int32, (width, width), 1) // hd
    same_head = jnp.where(lane_i == lane_j, 1.0, 0.0).astype(BF16)
    row_head = lax.broadcasted_iota(jnp.int32, (rows, width), 1) // hd

    normed = x * lax.rsqrt(jnp.mean(x * x, -1, keepdims=True) + EPSILON) * gain
    packed = dot3(split(normed), w_qkv)
    q, k, v = packed[:, :width], packed[:, width : 2 * width], packed[:, 2 * width :]
    q = q * lax.rsqrt(dot2(split(q * q), same_head) + EPSILON) * ATTN_SCALE
    k = k * lax.rsqrt(dot2(split(k * k), same_head) + EPSILON)
    qh, ql = split(q)
    ks = split(k)
    vh, vl = split(v)
    mixed = None
    for h in range(HEADS):
        mine = jnp.where(row_head == h, 1.0, 0.0).astype(BF16)
        e = jnp.exp(dot3((qh * mine, ql * mine), ks, NT))
        if mask is not None:
            e = e * mask
        es = split(e)
        o = dot3(es, (vh * mine, vl * mine))
        t = dot2(es, mine)
        mixed, totals = (o, t) if h == 0 else (mixed + o, totals + t)
    return x + dot3(split(mixed / totals), w_out)


def body(
    n,
    video,
    starts,
    gain_space,
    qkv_space,
    out_space,
    gain_time,
    qkv_time,
    out_time,
    code_sums,
    code_counts,
    latents,
    terms,
    acc,
    spaced,
    xin,
    codes,
    weights,
    u_hi,
    u_lo,
    cs,
    ck,
    cr,
    ys,
    yr,
    zs,
    zr,
    a2a_send,
    a2a_recv,
    gz_send,
    gz_recv,
    gy_send,
    gy_recv,
    gc_send,
    gc_recv,
    rc_send,
    rc_recv,
    ry_send,
    ry_recv,
    rz_send,
    rz_recv,
):
    clips, places, width = video.shape
    share = places // n
    rows = code_sums.shape[0]
    n4 = n // 4
    halves = ck.shape[1]
    part = rows // halves
    tokens = clips * places

    me = lax.axis_index("frames")
    zz, b1, b0 = me // 4, (me // 2) % 2, me % 2
    y_mate = zz * 4 + (1 - b1) * 2 + b0
    c_mate = zz * 4 + b1 * 2 + (1 - b0)
    pending = []

    def remote(src, dst, ssem, rsem, dev):
        return pltpu.make_async_remote_copy(
            src_ref=src, dst_ref=dst, send_sem=ssem, recv_sem=rsem,
            device_id={"frames": dev}, device_id_type=pl.DeviceIdType.MESH,
        )

    def send(src, dst, ssem, rsem, dev):
        cp = remote(src, dst, ssem, rsem, dev)
        cp.start()
        pending.append(cp)

    barrier = pltpu.get_barrier_semaphore()

    def greet(i, c):
        pl.semaphore_signal(
            barrier, inc=1, device_id={"frames": lax.rem(me + i, n)},
            device_id_type=pl.DeviceIdType.MESH,
        )
        return c

    lax.fori_loop(1, n, greet, 0)

    own = code_sums[...] / jnp.transpose(jnp.broadcast_to(code_counts[...], (width, rows)))
    own = own * lax.rsqrt(jnp.sum(own * own, -1, keepdims=True) + EPSILON)
    codes[me] = own
    pl.semaphore_wait(barrier, n - 1)

    def block(d, y, c):
        return lax.rem(zz + d, n4) * 4 + y * 2 + c

    def reach(side, s):
        at = zz - s if side == 0 else zz + s
        return at, (at >= 0 if side == 0 else at < n4)

    def slot(side, s):
        return 0 if s == 0 else side * (n4 - 1) + s

    def each(s, do):
        if s == 0:
            do(0, 0)
        else:
            for side in range(2):
                pl.when(reach(side, s)[1])(functools.partial(do, side, s))

    def copy_of(g, ssem, rsem, k, dev):
        return remote(codes.at[g], codes.at[g], ssem.at[k], rsem.at[k], dev)

    def own_block(side, s):
        return reach(side, s)[0] * 4 + b1 * 2 + b0

    def y_block(side, s):
        return reach(side, s)[0] * 4 + (1 - b1) * 2 + b0

    def along(side, s):
        ahead, there = reach(1 - side, 1)
        k = side * n4 + s + 1
        return copy_of(own_block(side, s), gz_send, gz_recv, k, ahead * 4 + b1 * 2 + b0), there

    def forward_own(s):
        def do(side, s):
            g = own_block(side, s)
            if s:
                copy_of(g, gz_send, gz_recv, side * n4 + s, me).wait_recv()
            for sd in range(2) if s == 0 else (side,):
                if s + 1 < n4:
                    cp, there = along(sd, s)
                    pl.when(there)(cp.start)
            k = slot(side, s)
            copy_of(g, gy_send, gy_recv, k, y_mate).start()
            copy_of(g, gc_send, gc_recv, k, c_mate).start()

        each(s, do)

    def forward_y(s):
        def do(side, s):
            g, k = y_block(side, s), slot(side, s)
            copy_of(g, gy_send, gy_recv, k, me).wait_recv()
            copy_of(g, gc_send, gc_recv, 2 * n4 + k, c_mate).start()

        each(s, do)

    def gather_sent(s):
        def do(side, s):
            for sd in range(2) if s == 0 else (side,):
                if s + 1 < n4:
                    cp, there = along(sd, s)
                    pl.when(there)(cp.wait_send)
            g, k = own_block(side, s), slot(side, s)
            copy_of(g, gy_send, gy_recv, k, y_mate).wait_send()
            copy_of(g, gc_send, gc_recv, k, c_mate).wait_send()
            g = y_block(side, s)
            copy_of(g, gc_send, gc_recv, 2 * n4 + k, c_mate).wait_send()

        each(s, do)

    forward_own(0)

    w_q, w_o = split(qkv_space[...]), split(out_space[...])
    gain = gain_space[...]
    for c in range(clips):
        spaced[c] = attention(video[c], gain, w_q, w_o, None)
        for d in range(1, n):
            to = lax.rem(me + d, n)
            send(
                spaced.at[c, pl.ds(pl.multiple_of(to * share, 8), share), :],
                xin.at[c, me], a2a_send.at[c, d], a2a_recv.at[c, d], to,
            )
        xin[c, me] = spaced[c, pl.ds(pl.multiple_of(me * share, 8), share), :]
    if n4 > 1:
        forward_own(1)

    w_q, w_o = split(qkv_time[...]), split(out_time[...])
    gain = gain_time[...]
    bits = share.bit_length() - 1
    r_i = lax.broadcasted_iota(jnp.int32, (places, places), 0)
    r_j = lax.broadcasted_iota(jnp.int32, (places, places), 1)
    t_i, t_j = r_i >> bits, r_j >> bits
    same_place = (r_i & (share - 1)) == (r_j & (share - 1))
    for c in range(clips):
        if c == 1:
            forward_y(0)
        for d in range(1, n):
            src = lax.rem(me + n - d, n)
            remote(xin.at[c, src], xin.at[c, src], a2a_send.at[c, d], a2a_recv.at[c, d], me).wait_recv()
        allowed = same_place & (t_j <= t_i) & ((t_j >= starts[c]) | (t_j == t_i))
        mask = jnp.where(allowed, 1.0, 0.0)
        y = attention(xin[c].reshape(places, width), gain, w_q, w_o, mask)
        latents[c] = y.reshape(n, share, width)
        u = y * lax.rsqrt(jnp.sum(y * y, -1, keepdims=True) + EPSILON)
        u_hi[0, pl.ds(c * places, places), :], u_lo[0, pl.ds(c * places, places), :] = split(u)
        u = u * (1.0 / SOFTMAX_WARMTH)
        u_hi[1, pl.ds(c * places, places), :], u_lo[1, pl.ds(c * places, places), :] = split(u)
    if clips == 1:
        forward_y(0)

    def score(g):
        e = jnp.exp(dot3(split(codes[g]), (u_hi[1], u_lo[1]), NT))
        weights[g] = e
        acc[...] += jnp.sum(e.reshape(rows // 8, 8, tokens), 0)

    def score_all(s):
        def do(side, s):
            at, k = reach(side, s)[0], slot(side, s)
            for y, k in ((b1, k), (1 - b1, 2 * n4 + k)):
                copy_of(at * 4 + y * 2 + (1 - b0), gc_send, gc_recv, k, me).wait_recv()

            def one(i, carry):
                score(at * 4 + i)
                return carry

            lax.fori_loop(0, 4, one, 0)

        each(s, do)

    acc[...] = jnp.zeros((8, tokens), F32)
    for s in range(2, n4 + 2):
        if s < n4:
            forward_own(s)
        if s - 1 < n4:
            forward_y(s - 1)
        score_all(s - 2)
    inv = 1.0 / jnp.sum(acc[...], 0, keepdims=True)
    ones = jnp.ones((8, tokens), BF16)

    def term(g, h, dst):
        ps = split(weights[g, pl.ds(h * part, part), :] * inv)
        dst[pl.ds(0, part), :] = dot3(ps, (u_hi[0], u_lo[0]))
        cnt = dot(ones, ps[0], NT) + dot(ones, ps[1], NT)
        if part < width:
            cnt = jnp.concatenate([cnt, jnp.zeros((8, width - part), F32)], 1)
        dst[pl.ds(part, 8), :] = cnt

    def start(d, h):
        for j in range(2):
            y = lax.rem(b1 + 1 + j, 2)
            term(block(d, y, 1 - b0), h, cs.at[d, h, j])
            send(cs.at[d, h, j], cr.at[d, h, j], rc_send.at[d, h, j], rc_recv.at[d, h, j], c_mate)
        for j in range(2):
            y = lax.rem(b1 + 1 + j, 2)
            term(block(d, y, b0), h, ck.at[d, h, j])

    def wait_core(d, h, j):
        remote(cr.at[d, h, j], cr.at[d, h, j], rc_send.at[d, h, j], rc_recv.at[d, h, j], me).wait_recv()

    def pair(d, h):
        wait_core(d, h, 0)
        ys[d, h] = ck[d, h, 0] + cr[d, h, 0]
        send(ys.at[d, h], yr.at[d, h], ry_send.at[d, h], ry_recv.at[d, h], y_mate)

    def across(d, h):
        wait_core(d, h, 1)
        remote(yr.at[d, h], yr.at[d, h], ry_send.at[d, h], ry_recv.at[d, h], me).wait_recv()
        zs[d, h] = ck[d, h, 1] + cr[d, h, 1] + yr[d, h]
        if d:
            send(zs.at[d, h], zr.at[d, h], rz_send.at[d, h], rz_recv.at[d, h], block(d, b1, b0))

    steps = [(d % n4, h) for d in range(1, n4 + 1) for h in range(halves)]
    total = len(steps)
    for i in range(total + 2):
        if i < total:
            start(*steps[i])
        if 1 <= i <= total:
            pair(*steps[i - 1])
        if i >= 2:
            across(*steps[i - 2])

    for h in range(halves):
        tot = zs[0, h]
        for d in range(1, n4):
            remote(zr.at[d, h], zr.at[d, h], rz_send.at[d, h], rz_recv.at[d, h], me).wait_recv()
            tot = tot + zr[d, h]
        terms[h] = tot
    for s in range(n4):
        gather_sent(s)
    for cp in pending:
        cp.wait_send()


def finish(found, terms, code_sums, code_counts, latents, new_sums, new_counts, new_codebook):
    halves, high, width = terms.shape
    part = high - 8
    latents[...] = found[...]
    for h in range(halves):
        tot = terms[h]
        span = pl.ds(h * part, part)
        sums = DECAY_RATE * code_sums[span, :] + (1.0 - DECAY_RATE) * tot[:part]
        counts = DECAY_RATE * code_counts[:, span] + (1.0 - DECAY_RATE) * tot[part : part + 1, :part]
        new_sums[span, :] = sums
        new_counts[:, span] = counts
        new_codebook[span, :] = sums / jnp.transpose(jnp.broadcast_to(counts, (width, part)))


def local(n, video, clip_start, gain_space, qkv_space, out_space, gain_time, qkv_time, out_time, code_sums, code_counts):
    clips, _, places, width = video.shape
    rows = code_sums.shape[0]
    share, n4 = places // n, n // 4
    halves = 2 if rows >= 256 else 1
    high = rows // halves + 8
    tokens = clips * places
    vmem = pl.BlockSpec(memory_space=pltpu.VMEM)
    dma = pltpu.SemaphoreType.DMA
    found, terms = pl.pallas_call(
        functools.partial(body, n),
        out_shape=(
            jax.ShapeDtypeStruct((clips, n, share, width), F32),
            jax.ShapeDtypeStruct((halves, high, width), F32),
        ),
        in_specs=[vmem, pl.BlockSpec(memory_space=pltpu.SMEM)] + [vmem] * 8,
        out_specs=(vmem,) * 2,
        scratch_shapes=[
            pltpu.VMEM((8, tokens), F32),
            pltpu.VMEM((clips, places, width), F32),
            pltpu.VMEM((clips, n, share, width), F32),
            pltpu.VMEM((n, rows, width), F32),
            pltpu.VMEM((n, rows, tokens), F32),
            pltpu.VMEM((2, tokens, width), BF16),
            pltpu.VMEM((2, tokens, width), BF16),
            pltpu.VMEM((n4, halves, 2, high, width), F32),
            pltpu.VMEM((n4, halves, 2, high, width), F32),
            pltpu.VMEM((n4, halves, 2, high, width), F32),
            pltpu.VMEM((n4, halves, high, width), F32),
            pltpu.VMEM((n4, halves, high, width), F32),
            pltpu.VMEM((n4, halves, high, width), F32),
            pltpu.VMEM((n4, halves, high, width), F32),
            dma((clips, n)), dma((clips, n)),
            dma((2 * n4,)), dma((2 * n4,)),
            dma((2 * n4,)), dma((2 * n4,)),
            dma((4 * n4,)), dma((4 * n4,)),
            dma((n4, halves, 2)), dma((n4, halves, 2)),
            dma((n4, halves)), dma((n4, halves)),
            dma((n4, halves)), dma((n4, halves)),
        ],
        compiler_params=pltpu.CompilerParams(
            collective_id=0, has_side_effects=True, vmem_limit_bytes=60 * 2**20
        ),
        name="tokenizer",
    )(
        video.reshape(clips, places, width), clip_start, gain_space.reshape(1, -1), qkv_space, out_space,
        gain_time.reshape(1, -1), qkv_time, out_time, code_sums, code_counts.reshape(1, -1),
    )
    lat, sums, counts, book = pl.pallas_call(
        finish,
        out_shape=(
            jax.ShapeDtypeStruct((clips, n, share, width), F32),
            jax.ShapeDtypeStruct((rows, width), F32),
            jax.ShapeDtypeStruct((1, rows), F32),
            jax.ShapeDtypeStruct((rows, width), F32),
        ),
        in_specs=[vmem] * 4,
        out_specs=(vmem,) * 4,
        name="finish",
    )(found, terms, code_sums, code_counts.reshape(1, -1))
    return lat, sums, counts.reshape(rows), book


def solution(mesh):
    in_specs = (
        P("groups", "frames", None, None),
        P("groups"),
        P(),
        P(),
        P(),
        P(),
        P(),
        P(),
        P(("groups", "frames"), None),
        P(("groups", "frames")),
    )
    out_specs = (
        P("groups", None, "frames", None),
        P(("groups", "frames"), None),
        P(("groups", "frames")),
        P(("groups", "frames"), None),
    )
    fn = functools.partial(local, mesh.shape["frames"])
    return jax.shard_map(fn, mesh=mesh, in_specs=in_specs, out_specs=out_specs, check_vma=False)
```

profile of v0, /device:TPU:10, one launch (start us, length us, event | category | flops | bytes accessed | tf_op | source)
XLA Modules:
  0.0 84.8 jit_solution(10850424458391860356)
XLA Ops:
  0.6 81.9 %tokenizer.1 = (f32[2,16,16,256]{3,2,1,0:T(8,128)}, f32[2,136,256]{2,1,0:T(8,128)}) custom-call(f32[2,256,256]{2,1,0:T(8,128)} %bitcast.5, s32[2]{0:T(128)} %starts.1, f32[1,256]{1,0:T(1,128)} %bitcast.8, f32[256,768]{1,0:T(8,128)} %qkv_space.1, f32[256,256]{1,0:T(8,128)} %out_space.1, f32[1,256]{1,0:T(1,128)} %bitcast.9, f32[256,768]{1,0:T(8,128)} %qkv_time.1, ...), custom_call_target="tpu_custom_call" | custom-call | tf_op jit(solution)/shard_map/tokenizer/pallas_call | solution.py:365
  82.6 2.2 %finish.1 = (f32[2,16,16,256]{3,2,1,0:T(8,128)}, f32[256,256]{1,0:T(8,128)}, f32[1,256]{1,0:T(1,128)}, f32[256,256]{1,0:T(8,128)}) custom-call(f32[2,16,16,256]{3,2,1,0:T(8,128)} %get-tuple-element.10.found, f32[2,136,256]{2,1,0:T(8,128)} %get-tuple-element.11.terms, f32[256,256]{1,0:T(8,128)} %code_sums.3, f32[1,256]{1,0:T(1,128)} %bitcast.7), custom_call_target="tpu_custom_call" | custom-call | tf_op jit(solution)/shard_map/finish/pallas_call | solution.py:404
where the time goes:
time: 85 us; the launch traced here: 84.8 us
  Pallas kernels  84.1 us (99%)
    pallas_call x1, Pallas kernels, local(): pl.pallas_call(functools.partial(body, n), out_shape=(jax.ShapeDtypeStruc...  81.9 us
    pallas_call x1, Pallas kernels, local(): pl.pallas_call(finish, out_shape=(jax.ShapeDtypeStruct((clips, n, share,...  2.21 us

commit v1 on v0

v1 whole, which is shorter than its diff:
```python
import functools

import jax
import jax.numpy as jnp
from jax import lax
from jax.experimental import pallas as pl
from jax.experimental.pallas import tpu as pltpu
from jax.sharding import PartitionSpec as P

HEADS = 4
ATTN_SCALE = 10.0
SOFTMAX_WARMTH = 0.05
DECAY_RATE = 0.9
EPSILON = 1e-06
F32 = jnp.float32
BF16 = jnp.bfloat16
NN = (((1,), (0,)), ((), ()))
NT = (((1,), (1,)), ((), ()))


def split(a):
    hi = a.astype(BF16)
    return hi, (a - hi.astype(F32)).astype(BF16)


def dot(a, b, dims=NN):
    return lax.dot_general(a, b, dims, preferred_element_type=F32)


def dot3(a, b, dims=NN):
    return dot(a[0], b[0], dims) + (dot(a[0], b[1], dims) + dot(a[1], b[0], dims))


def dot2(a, b, dims=NN):
    return dot(a[0], b, dims) + dot(a[1], b, dims)


def attention(x, gain, w_qkv, w_out, mask):
    rows, width = x.shape
    hd = width // HEADS
    pair = 2 * hd
    lane_i = lax.broadcasted_iota(jnp.int32, (width, width), 0) // hd
    lane_j = lax.broadcasted_iota(jnp.int32, (width, width), 1) // hd
    same_head = jnp.where(lane_i == lane_j, 1.0, 0.0).astype(BF16)
    first = lax.broadcasted_iota(jnp.int32, (rows, pair), 1) < hd

    def product(a, w):
        ah, al = split(a)
        both = dot(jnp.concatenate([ah, al], 0), w[0])
        return both[:rows] + (both[rows:] + dot(ah, w[1]))

    normed = x * lax.rsqrt(jnp.mean(x * x, -1, keepdims=True) + EPSILON) * gain
    packed = product(normed, w_qkv)
    q, k, v = packed[:, :width], packed[:, width : 2 * width], packed[:, 2 * width :]
    squares = dot(jnp.concatenate(split(q * q) + split(k * k), 0), same_head)
    q = q * lax.rsqrt(squares[:rows] + squares[rows : 2 * rows] + EPSILON) * ATTN_SCALE
    k = k * lax.rsqrt(squares[2 * rows : 3 * rows] + squares[3 * rows :] + EPSILON)
    mixed = []
    for p in range(HEADS // 2):
        at = slice(p * pair, (p + 1) * pair)
        qh = q[:, at].astype(BF16).astype(F32)
        kh = k[:, at].astype(BF16).astype(F32)
        ql = pltpu.roll(q[:, at] - qh, hd, 1)
        kr = pltpu.roll(kh, hd, 1)
        kl = k[:, at] - kh
        s_a = dot(
            jnp.concatenate([jnp.where(first, qh, ql), jnp.where(first, qh, 0.0)], 1).astype(BF16),
            jnp.concatenate([jnp.where(first, kh, kr), kl], 1).astype(BF16), NT,
        )
        s_b = dot(
            jnp.concatenate([jnp.where(first, ql, qh), jnp.where(first, 0.0, qh)], 1).astype(BF16),
            jnp.concatenate([jnp.where(first, kr, kh), kl], 1).astype(BF16), NT,
        )
        e_a, e_b = jnp.exp(s_a), jnp.exp(s_b)
        if mask is not None:
            e_a, e_b = e_a * mask, e_b * mask
        e = jnp.concatenate([e_a, e_b], 0)
        eh, el = split(e)
        vh, vl = split(v[:, at])
        o = dot(eh, jnp.concatenate([vh, vl], 1))
        o = o[:, :pair] + (o[:, pair:] + dot(el, vh))
        o = o / jnp.sum(e, -1, keepdims=True)
        mixed.append(jnp.where(first, o[:rows], o[rows:]))
    return x + product(jnp.concatenate(mixed, 1), w_out)


def body(
    n,
    parts,
    video,
    starts,
    gain_space,
    qkv_space,
    out_space,
    gain_time,
    qkv_time,
    out_time,
    code_sums,
    code_counts,
    latents,
    terms,
    spaced,
    xin,
    codes,
    tok,
    weights,
    unit,
    warm,
    total,
    den,
    counted,
    part_sums,
    arrived,
    a2a_send,
    a2a_recv,
    g_send,
    g_recv,
    t_send,
    t_recv,
    d_send,
    d_recv,
    r_send,
    r_recv,
):
    clips, places, width = video.shape
    share = places // n
    pieces = xin.shape[1]
    rows = code_sums.shape[0]
    blocks = codes.shape[0]
    mates = tok.shape[1]
    stages = blocks.bit_length() - 1
    tokens = mates * places
    chunk, part, lanes = rows // 4, rows // parts, 128
    code_bits = [1] + list(range(3, n.bit_length() - 1))

    me = lax.axis_index("frames")
    pending = []

    def flip(k):
        return (1 - 2 * ((me // 2**k) % 2)) * 2**k

    def token_mate(k):
        return me + (k & 1) * flip(0) + (k >> 1) * flip(2)

    def block_mate(r):
        to = me
        for j in range(stages):
            if (r >> j) & 1:
                to = to + flip(code_bits[j])
        return to

    def remote(src, dst, ssem, rsem, dev):
        return pltpu.make_async_remote_copy(
            src_ref=src, dst_ref=dst, send_sem=ssem, recv_sem=rsem,
            device_id={"frames": dev}, device_id_type=pl.DeviceIdType.MESH,
        )

    def send(src, dst, ssem, rsem, dev):
        cp = remote(src, dst, ssem, rsem, dev)
        cp.start()
        pending.append(cp)

    barrier = pltpu.get_barrier_semaphore()

    def greet(i, c):
        pl.semaphore_signal(
            barrier, inc=1, device_id={"frames": lax.rem(me + i, n)},
            device_id_type=pl.DeviceIdType.MESH,
        )
        return c

    lax.fori_loop(1, n, greet, 0)

    own = code_sums[...] / jnp.transpose(jnp.broadcast_to(code_counts[...], (width, rows)))
    codes[0] = own * lax.rsqrt(jnp.sum(own * own, -1, keepdims=True) + EPSILON)
    pl.semaphore_wait(barrier, n - 1)

    def code_copy(r, q, ch, dev):
        at = pl.ds(ch * chunk, chunk)
        return remote(codes.at[r, at], codes.at[q, at], g_send.at[q, ch], g_recv.at[q, ch], dev)

    def give_codes(r, j, ch):
        cp = code_copy(r, r ^ (1 << j), ch, block_mate(1 << j))
        cp.start()
        pending.append(cp)

    def await_codes(r, chs):
        for ch in chs:
            code_copy(r, r, ch, me).wait_recv()

    def pass_codes(chs):
        for j in range(1, stages):
            for r in range(1 << j, 2 << j, 2):
                for ch in chs:
                    await_codes(r, [ch])
                    for i in range(j + 1, stages):
                        give_codes(r, i, ch)
                    give_codes(r, 0, ch)

    def token_copy(c, h, q, p, dev):
        at = pl.ds(h * (places // pieces), places // pieces)
        return remote(tok.at[c, q, at], tok.at[c, p, at], t_send.at[c, h, p], t_recv.at[c, h, p], dev)

    def give_tokens(c, h, q, k, dev):
        cp = token_copy(c, h, q, q ^ k, dev)
        cp.start()
        pending.append(cp)

    def await_tokens(c, h, q):
        token_copy(c, h, q, q, me).wait_recv()

    early, late = [0], [1, 2, 3]
    for ch in early + late:
        give_codes(0, 0, ch)
    for ch in early:
        for j in range(1, stages):
            give_codes(0, j, ch)

    w_q, w_o = split(qkv_space[...]), split(out_space[...])
    gain = gain_space[...]
    def deal(c, h, d):
        to = lax.rem(me + d, n)
        send(
            spaced.at[c, pl.ds(pl.multiple_of(to * share + h * places // n // pieces, 8), share // pieces), :],
            xin.at[c, h, me], a2a_send.at[c, h, d], a2a_recv.at[c, h, d], to,
        )

    def await_deal(c, h, d):
        src = lax.rem(me + n - d, n)
        remote(xin.at[c, h, src], xin.at[c, h, src], a2a_send.at[c, h, d], a2a_recv.at[c, h, d], me).wait_recv()

    def keep(c):
        for h in range(pieces):
            at = pl.ds(pl.multiple_of(me * share + h * places // n // pieces, 8), share // pieces)
            xin[c, h, me] = spaced[c, at, :]

    units = [(c, h) for c in range(clips) for h in range(pieces)]
    for c in range(clips):
        spaced[c] = attention(video[c], gain, w_q, w_o, None)
        if c < 2:
            for d in range(1, n):
                deal(*units[c], d)
        keep(c)

    def ready(c, h):
        for q in (2 * h, 2 * h + 1):
            if q % 2:
                for i in range(pieces):
                    await_tokens(c, i, q)
            u = tok[c, q]
            at = pl.ds((c * mates + q) * places, places)
            unit[at, :] = u.astype(BF16)
            warm[0, at, :], warm[1, at, :] = split(u * (1.0 / SOFTMAX_WARMTH))

    def score(c, h, r):
        two = 2 * places
        at = pl.ds(c * tokens + h * two, two)
        e = jnp.exp(dot3(split(codes[r]), (warm[0, at, :], warm[1, at, :]), NT))
        at = pl.ds(h * two, two)
        weights[c, r, :, at] = e
        t = jnp.sum(e.reshape(rows // 8, 8, two), 0)
        total[c, :, at] = t if r == 0 else total[c, :, at] + t

    def share_totals(c):
        den[c, 0] = jnp.sum(total[c], 0, keepdims=True)
        for k in range(1, mates):
            send(den.at[c, 0], den.at[c, k], d_send.at[c, k], d_recv.at[c, k], token_mate(k))

    def inverse_totals(c):
        for k in range(1, mates):
            remote(den.at[c, k], den.at[c, k], d_send.at[c, k], d_recv.at[c, k], me).wait_recv()
        full = [
            sum(den[c, k, :, pl.ds((q ^ k) * places, places)] for k in range(mates)) for q in range(mates)
        ]
        return 1.0 / jnp.concatenate(full, 1)

    w_q, w_o = split(qkv_time[...]), split(out_time[...])
    gain = gain_time[...]
    block = places // pieces
    bits = (share // pieces).bit_length() - 1
    r_i = lax.broadcasted_iota(jnp.int32, (block, block), 0)
    r_j = lax.broadcasted_iota(jnp.int32, (block, block), 1)
    t_i, t_j = r_i >> bits, r_j >> bits
    same_place = (r_i & (share // pieces - 1)) == (r_j & (share // pieces - 1))

    def pass_tokens(c, h):
        await_tokens(c, h, 2)
        give_tokens(c, h, 2, 1, token_mate(1))

    def late_codes():
        for ch in late:
            for j in range(1, stages):
                give_codes(0, j, ch)

    for i, (c, h) in enumerate(units):
        for d in range(1, n):
            await_deal(c, h, d)
            if i + 2 < len(units):
                deal(*units[i + 2], d)
        allowed = same_place & (t_j <= t_i) & ((t_j >= starts[c]) | (t_j == t_i))
        mask = jnp.where(allowed, 1.0, 0.0)
        y = attention(xin[c, h].reshape(block, width), gain, w_q, w_o, mask)
        each = share // pieces
        latents[c, :, pl.ds(h * each, each), :] = y.reshape(n, each, width)
        tok[c, 0, pl.ds(h * block, block), :] = y * lax.rsqrt(jnp.sum(y * y, -1, keepdims=True) + EPSILON)
        give_tokens(c, h, 0, 2, token_mate(2))
        give_tokens(c, h, 0, 1, token_mate(1))
        if i >= 2:
            pass_tokens(*units[i - 2])
        if i == 0:
            late_codes()
    pass_codes(early)
    for i in range(len(units) - 2, len(units)):
        if units[i][0] == 0:
            pass_tokens(*units[i])
    ready(0, 0)
    await_codes(1, early + late)
    score(0, 0, 0)
    score(0, 0, 1)
    ready(1, 0)
    score(1, 0, 0)
    score(1, 0, 1)
    ready(0, 1)
    score(0, 1, 0)
    score(0, 1, 1)
    pass_codes(late)
    evens = range(2, blocks, 2)
    odds = range(3, blocks, 2)
    for r in evens:
        for c, h in ((0, 0), (0, 1), (1, 0)):
            score(c, h, r)
    for i in range(len(units) - 2, len(units)):
        if units[i][0]:
            pass_tokens(*units[i])
    for r in odds:
        await_codes(r, early + late)
        for c, h in ((0, 0), (0, 1), (1, 0)):
            score(c, h, r)
    share_totals(0)
    ready(1, 1)
    for r in range(blocks):
        score(1, 1, r)
    share_totals(1)
    ones = jnp.ones((8, lanes), BF16)

    def term(c, r, h, inv):
        first, size = h * part, part
        p = weights[c, r, pl.ds(first, size), :] * inv
        at = pl.ds(c * tokens, tokens)
        sums = dot(p.astype(BF16), unit[at, :])
        k = p[:, :lanes]
        for i in range(1, tokens // lanes):
            k = k + p[:, i * lanes : (i + 1) * lanes]
        at = pl.ds(first, size)
        if c:
            sums = part_sums[r, at, :] + sums
            k = counted[r, at, :] + k
        part_sums[r, at, :] = sums
        counted[r, at, :] = k
        if c == clips - 1 and first + size == rows:
            kh, kl = split(counted[r])
            cnt = dot(ones, kh, NT) + dot(ones, kl, NT)
            if rows < width:
                cnt = jnp.concatenate([cnt, jnp.zeros((8, width - rows), F32)], 1)
            part_sums[r, pl.ds(rows, 8), :] = cnt

    def stage_of(r):
        j = 0
        while j < stages and not (r >> j) & 1:
            j += 1
        return j

    def slot(r, j):
        return (blocks - (blocks >> j)) + (r >> (j + 1))

    order = sorted(range(blocks), key=lambda r: (stage_of(r), -r))
    inv = inverse_totals(0)
    for c in range(clips - 1):
        for r in order:
            for h in range(parts):
                term(c, r, h, inv)
        inv = inverse_totals(c + 1)
    for r in order:
        k = stage_of(r)
        for h in range(parts):
            term(clips - 1, r, h, inv)
            at = pl.ds(h * part, part + (8 if h == parts - 1 else 0))
            for j in range(k):
                i = slot(r, j)
                remote(arrived.at[i, at], arrived.at[i, at], r_send.at[i, h], r_recv.at[i, h], me).wait_recv()
                part_sums[r, at, :] = part_sums[r, at, :] + arrived[i, at, :]
            if r:
                i = slot(r ^ (1 << k), k)
                send(part_sums.at[r, at], arrived.at[i, at], r_send.at[i, h], r_recv.at[i, h], block_mate(1 << k))
            else:
                terms[at, :] = part_sums[r, at, :]
    for cp in pending:
        cp.wait_send()


def finish(found, terms, code_sums, code_counts, latents, new_sums, new_counts, new_codebook):
    rows, width = code_sums.shape
    latents[...] = found[...]
    sums = DECAY_RATE * code_sums[...] + (1.0 - DECAY_RATE) * terms[:rows, :]
    counts = DECAY_RATE * code_counts[...] + (1.0 - DECAY_RATE) * terms[rows : rows + 1, :rows]
    new_sums[...] = sums
    new_counts[...] = counts
    new_codebook[...] = sums / jnp.transpose(jnp.broadcast_to(counts, (width, rows)))


def local(n, video, clip_start, gain_space, qkv_space, out_space, gain_time, qkv_time, out_time, code_sums, code_counts):
    clips, _, places, width = video.shape
    rows = code_sums.shape[0]
    share, blocks, mates = places // n, n // 4, 4
    parts = max(1, rows // 64)
    pieces = 1
    tokens = mates * places
    vmem = pl.BlockSpec(memory_space=pltpu.VMEM)
    dma = pltpu.SemaphoreType.DMA
    found, terms = pl.pallas_call(
        functools.partial(body, n, parts),
        out_shape=(
            jax.ShapeDtypeStruct((clips, n, share, width), F32),
            jax.ShapeDtypeStruct((rows + 8, width), F32),
        ),
        in_specs=[vmem, pl.BlockSpec(memory_space=pltpu.SMEM)] + [vmem] * 8,
        out_specs=(vmem,) * 2,
        scratch_shapes=[
            pltpu.VMEM((clips, places, width), F32),
            pltpu.VMEM((clips, pieces, n, share // pieces, width), F32),
            pltpu.VMEM((blocks, rows, width), F32),
            pltpu.VMEM((clips, mates, places, width), F32),
            pltpu.VMEM((clips, blocks, rows, tokens), F32),
            pltpu.VMEM((clips * tokens, width), BF16),
            pltpu.VMEM((2, clips * tokens, width), BF16),
            pltpu.VMEM((clips, 8, tokens), F32),
            pltpu.VMEM((clips, mates, 1, tokens), F32),
            pltpu.VMEM((blocks, rows, 128), F32),
            pltpu.VMEM((blocks, rows + 8, width), F32),
            pltpu.VMEM((blocks, rows + 8, width), F32),
            dma((clips, pieces, n)), dma((clips, pieces, n)),
            dma((blocks, 4)), dma((blocks, 4)),
            dma((clips, pieces, mates)), dma((clips, pieces, mates)),
            dma((clips, mates)), dma((clips, mates)),
            dma((blocks, parts)), dma((blocks, parts)),
        ],
        compiler_params=pltpu.CompilerParams(
            collective_id=0, has_side_effects=True, vmem_limit_bytes=60 * 2**20
        ),
        name="tokenizer",
    )(
        video.reshape(clips, places, width), clip_start, gain_space.reshape(1, -1), qkv_space, out_space,
        gain_time.reshape(1, -1), qkv_time, out_time, code_sums, code_counts.reshape(1, -1),
    )
    lat, sums, counts, book = pl.pallas_call(
        finish,
        out_shape=(
            jax.ShapeDtypeStruct((clips, n, share, width), F32),
            jax.ShapeDtypeStruct((rows, width), F32),
            jax.ShapeDtypeStruct((1, rows), F32),
            jax.ShapeDtypeStruct((rows, width), F32),
        ),
        in_specs=[vmem] * 4,
        out_specs=(vmem,) * 4,
        name="finish",
    )(found, terms, code_sums, code_counts.reshape(1, -1))
    return lat, sums, counts.reshape(rows), book


def solution(mesh):
    in_specs = (
        P("groups", "frames", None, None),
        P("groups"),
        P(),
        P(),
        P(),
        P(),
        P(),
        P(),
        P(("groups", "frames"), None),
        P(("groups", "frames")),
    )
    out_specs = (
        P("groups", None, "frames", None),
        P(("groups", "frames"), None),
        P(("groups", "frames")),
        P(("groups", "frames"), None),
    )
    fn = functools.partial(local, mesh.shape["frames"])
    return jax.shard_map(fn, mesh=mesh, in_specs=in_specs, out_specs=out_specs, check_vma=False)
```

time: 85 us -> 69.4 us (0.82)
  the two profiles are of different devices: /device:TPU:10 before, /device:TPU:0 now
where the time goes in v1:
time: 69.4 us; the launch traced here: 69.2 us
  Pallas kernels  68.6 us (99%)
    pallas_call x1, Pallas kernels, local(): pl.pallas_call(functools.partial(body, n, parts), out_shape=(jax.ShapeDty...  66.4 us
    pallas_call x1, Pallas kernels, local(): pl.pallas_call(finish, out_shape=(jax.ShapeDtypeStruct((clips, n, share,...  2.21 us

profile of v1, /device:TPU:0, one launch (start us, length us, event | category | flops | bytes accessed | tf_op | source)
XLA Modules:
  0.0 69.2 jit_solution(15057230052104546691)
XLA Ops:
  0.6 66.4 %tokenizer.1 = (f32[2,16,16,256]{3,2,1,0:T(8,128)}, f32[264,256]{1,0:T(8,128)}) custom-call(f32[2,256,256]{2,1,0:T(8,128)} %bitcast.5, s32[2]{0:T(128)} %starts.1, f32[1,256]{1,0:T(1,128)} %bitcast.8, f32[256,768]{1,0:T(8,128)} %qkv_space.1, f32[256,256]{1,0:T(8,128)} %out_space.1, f32[1,256]{1,0:T(1,128)} %bitcast.9, f32[256,768]{1,0:T(8,128)} %qkv_time.1, ...), custom_call_target="tpu_custom_call" | custom-call | tf_op jit(solution)/shard_map/tokenizer/pallas_call | solution.py:420
  67.0 2.2 %finish.1 = (f32[2,16,16,256]{3,2,1,0:T(8,128)}, f32[256,256]{1,0:T(8,128)}, f32[1,256]{1,0:T(1,128)}, f32[256,256]{1,0:T(8,128)}) custom-call(f32[2,16,16,256]{3,2,1,0:T(8,128)} %get-tuple-element.10.found, f32[264,256]{1,0:T(8,128)} %get-tuple-element.11.terms, f32[256,256]{1,0:T(8,128)} %code_sums.3, f32[1,256]{1,0:T(1,128)} %bitcast.7), custom_call_target="tpu_custom_call" | custom-call | tf_op jit(solution)/shard_map/finish/pallas_call | solution.py:455

commit v2 on v1

--- a/solution.py
+++ b/solution.py
@@ -35,7 +35,7 @@
     return dot(a[0], b, dims) + dot(a[1], b, dims)
 
 
-def attention(x, gain, w_qkv, w_out, mask):
+def attention(x, gain, w_qkv, w_out, mask, between=None):
     rows, width = x.shape
     hd = width // HEADS
     pair = 2 * hd
@@ -55,6 +55,8 @@
     squares = dot(jnp.concatenate(split(q * q) + split(k * k), 0), same_head)
     q = q * lax.rsqrt(squares[:rows] + squares[rows : 2 * rows] + EPSILON) * ATTN_SCALE
     k = k * lax.rsqrt(squares[2 * rows : 3 * rows] + squares[3 * rows :] + EPSILON)
+    if between is not None:
+        between()
     mixed = []
     for p in range(HEADS // 2):
         at = slice(p * pair, (p + 1) * pair)
@@ -86,19 +88,29 @@
 
 def body(
     n,
-    parts,
-    video,
+    spans,
+    video_in,
     starts,
     gain_space,
+    qkv_space_in,
+    out_space_in,
+    gain_time,
+    qkv_time_in,
+    out_time_in,
+    code_sums_in,
+    code_counts,
+    latents_out,
+    terms_out,
+    video,
     qkv_space,
     out_space,
-    gain_time,
     qkv_time,
     out_time,
     code_sums,
-    code_counts,
     latents,
-    terms,
+    in_sem,
+    lat_sem,
+    out_sem,
     spaced,
     xin,
     codes,
@@ -130,7 +142,8 @@
     mates = tok.shape[1]
     stages = blocks.bit_length() - 1
     tokens = mates * places
-    chunk, part, lanes = rows // 4, rows // parts, 128
+    chunk, lanes = rows // 4, 128
+    parts, swapped = len(spans), 1 if stages > 1 else 0
     code_bits = [1] + list(range(3, n.bit_length() - 1))
 
     me = lax.axis_index("frames")
@@ -170,10 +183,15 @@
         return c
 
     lax.fori_loop(1, n, greet, 0)
-
-    own = code_sums[...] / jnp.transpose(jnp.broadcast_to(code_counts[...], (width, rows)))
-    codes[0] = own * lax.rsqrt(jnp.sum(own * own, -1, keepdims=True) + EPSILON)
-    pl.semaphore_wait(barrier, n - 1)
+    loads = {}
+    for i, (name, src, dst) in enumerate((
+        ("video0", video_in.at[0], video.at[0]), ("qkv_space", qkv_space_in, qkv_space),
+        ("out_space", out_space_in, out_space), ("code_sums", code_sums_in, code_sums),
+        ("video1", video_in.at[pl.ds(1, clips - 1)], video.at[pl.ds(1, clips - 1)]),
+        ("qkv_time", qkv_time_in, qkv_time), ("out_time", out_time_in, out_time),
+    )):
+        loads[name] = pltpu.make_async_copy(src, dst, in_sem.at[i])
+        loads[name].start()
 
     def code_copy(r, q, ch, dev):
         at = pl.ds(ch * chunk, chunk)
@@ -209,13 +227,27 @@
     def await_tokens(c, h, q):
         token_copy(c, h, q, q, me).wait_recv()
 
-    early, late = [0], [1, 2, 3]
-    for ch in early + late:
-        give_codes(0, 0, ch)
-    for ch in early:
-        for j in range(1, stages):
-            give_codes(0, j, ch)
-
+    code_at = [-2, -2, 0, 0]
+    early = [ch for ch in range(4) if code_at[ch] < 0]
+    late = [ch for ch in range(4) if code_at[ch] >= 0]
+
+    def across(when):
+        for ch in range(4 if when == -2 else 0):
+            give_codes(0, 0, ch)
+        for ch in range(4):
+            if code_at[ch] == when:
+                for j in range(1, stages):
+                    give_codes(0, j, ch)
+
+    def enter():
+        loads["code_sums"].wait()
+        own = code_sums[...] / jnp.transpose(jnp.broadcast_to(code_counts[...], (width, rows)))
+        codes[0] = own * lax.rsqrt(jnp.sum(own * own, -1, keepdims=True) + EPSILON)
+        pl.semaphore_wait(barrier, n - 1)
+        across(-2)
+
+    loads["qkv_space"].wait()
+    loads["out_space"].wait()
     w_q, w_o = split(qkv_space[...]), split(out_space[...])
     gain = gain_space[...]
     def deal(c, h, d):
@@ -236,11 +268,16 @@
 
     units = [(c, h) for c in range(clips) for h in range(pieces)]
     for c in range(clips):
-        spaced[c] = attention(video[c], gain, w_q, w_o, None)
         if c < 2:
+            loads["video%d" % c].wait()
+        spaced[c] = attention(video[c], gain, w_q, w_o, None, enter if c == 0 else None)
+        if c < 1:
             for d in range(1, n):
                 deal(*units[c], d)
         keep(c)
+    across(-1)
+    loads["qkv_time"].wait()
+    loads["out_time"].wait()
 
     def ready(c, h):
         for q in (2 * h, 2 * h + 1):
@@ -287,16 +324,12 @@
         await_tokens(c, h, 2)
         give_tokens(c, h, 2, 1, token_mate(1))
 
-    def late_codes():
-        for ch in late:
-            for j in range(1, stages):
-                give_codes(0, j, ch)
-
+    saves = []
     for i, (c, h) in enumerate(units):
         for d in range(1, n):
             await_deal(c, h, d)
-            if i + 2 < len(units):
-                deal(*units[i + 2], d)
+            if i + 1 < len(units):
+                deal(*units[i + 1], d)
         allowed = same_place & (t_j <= t_i) & ((t_j >= starts[c]) | (t_j == t_i))
         mask = jnp.where(allowed, 1.0, 0.0)
         y = attention(xin[c, h].reshape(block, width), gain, w_q, w_o, mask)
@@ -307,12 +340,11 @@
         give_tokens(c, h, 0, 1, token_mate(1))
         if i >= 2:
             pass_tokens(*units[i - 2])
-        if i == 0:
-            late_codes()
+        if h == pieces - 1:
+            saves.append(pltpu.make_async_copy(latents.at[c], latents_out.at[c], lat_sem.at[c]))
+            saves[-1].start()
+        across(i)
     pass_codes(early)
-    for i in range(len(units) - 2, len(units)):
-        if units[i][0] == 0:
-            pass_tokens(*units[i])
     ready(0, 0)
     await_codes(1, early + late)
     score(0, 0, 0)
@@ -320,23 +352,28 @@
     ready(1, 0)
     score(1, 0, 0)
     score(1, 0, 1)
-    ready(0, 1)
-    score(0, 1, 0)
-    score(0, 1, 1)
+    for i in range(len(units) - 2, len(units)):
+        if units[i][0] == 0:
+            pass_tokens(*units[i])
     pass_codes(late)
     evens = range(2, blocks, 2)
     odds = range(3, blocks, 2)
     for r in evens:
-        for c, h in ((0, 0), (0, 1), (1, 0)):
-            score(c, h, r)
+        score(0, 0, r)
+        score(1, 0, r)
+    ready(0, 1)
+    for r in (0, 1, *evens):
+        score(0, 1, r)
     for i in range(len(units) - 2, len(units)):
         if units[i][0]:
             pass_tokens(*units[i])
     for r in odds:
         await_codes(r, early + late)
-        for c, h in ((0, 0), (0, 1), (1, 0)):
-            score(c, h, r)
+        score(0, 0, r)
+        score(0, 1, r)
     share_totals(0)
+    for r in odds:
+        score(1, 0, r)
     ready(1, 1)
     for r in range(blocks):
         score(1, 1, r)
@@ -344,7 +381,7 @@
     ones = jnp.ones((8, lanes), BF16)
 
     def term(c, r, h, inv):
-        first, size = h * part, part
+        first, size = spans[h]
         p = weights[c, r, pl.ds(first, size), :] * inv
         at = pl.ds(c * tokens, tokens)
         sums = dot(p.astype(BF16), unit[at, :])
@@ -364,38 +401,60 @@
                 cnt = jnp.concatenate([cnt, jnp.zeros((8, width - rows), F32)], 1)
             part_sums[r, pl.ds(rows, 8), :] = cnt
 
-    def stage_of(r):
-        j = 0
-        while j < stages and not (r >> j) & 1:
-            j += 1
-        return j
-
-    def slot(r, j):
-        return (blocks - (blocks >> j)) + (r >> (j + 1))
-
-    order = sorted(range(blocks), key=lambda r: (stage_of(r), -r))
-    inv = inverse_totals(0)
-    for c in range(clips - 1):
-        for r in order:
-            for h in range(parts):
-                term(c, r, h, inv)
-        inv = inverse_totals(c + 1)
-    for r in order:
-        k = stage_of(r)
-        for h in range(parts):
-            term(clips - 1, r, h, inv)
-            at = pl.ds(h * part, part + (8 if h == parts - 1 else 0))
-            for j in range(k):
-                i = slot(r, j)
-                remote(arrived.at[i, at], arrived.at[i, at], r_send.at[i, h], r_recv.at[i, h], me).wait_recv()
-                part_sums[r, at, :] = part_sums[r, at, :] + arrived[i, at, :]
-            if r:
-                i = slot(r ^ (1 << k), k)
-                send(part_sums.at[r, at], arrived.at[i, at], r_send.at[i, h], r_recv.at[i, h], block_mate(1 << k))
-            else:
-                terms[at, :] = part_sums[r, at, :]
+    def route(h):
+        bits = list(range(stages))
+        return bits[1::-1] + bits[2:] if h < swapped else bits
+
+    def stage_of(r, h):
+        k = 0
+        while k < stages and not (r >> route(h)[k]) & 1:
+            k += 1
+        return k
+
+    def slot(r, k, h):
+        cleared = [sum(1 << j for j in route(h)[: i + 1]) for i in range(stages)]
+        places_at = [(i, q) for i in range(stages) for q in range(blocks) if not q & cleared[i]]
+        return places_at.index((k, r))
+
+    inv = {}
+    made = set()
+
+    def make(r, h, c):
+        if (r, h, c) not in made:
+            made.add((r, h, c))
+            if h == parts - 1 and c == clips - 1:
+                for g in range(h):
+                    make(r, g, c)
+            for b in range(c):
+                make(r, h, b)
+            if c not in inv:
+                inv[c] = inverse_totals(c)
+            term(c, r, h, inv[c])
+
+    jobs = [(r, h) for r in range(blocks) for h in range(parts)]
+    jobs.sort(key=lambda job: (stage_of(*job), -(job[1] < swapped) if stage_of(*job) == 0 else job[1] < swapped, -job[0], job[1]))
+    for r, h in jobs[: 2 * parts]:
+        make(r, h, 0)
+    for r, h in jobs:
+        make(r, h, clips - 1)
+        k = stage_of(r, h)
+        first, size = spans[h]
+        at = pl.ds(first, size + (8 if h == parts - 1 else 0))
+        for j in range(k):
+            i = slot(r, j, h)
+            remote(arrived.at[i, at], arrived.at[i, at], r_send.at[i, h], r_recv.at[i, h], me).wait_recv()
+            part_sums[r, at, :] = part_sums[r, at, :] + arrived[i, at, :]
+        if r:
+            j = route(h)[k]
+            i = slot(r ^ (1 << j), k, h)
+            send(part_sums.at[r, at], arrived.at[i, at], r_send.at[i, h], r_recv.at[i, h], block_mate(1 << j))
+        else:
+            saves.append(pltpu.make_async_copy(part_sums.at[r, at], terms_out.at[at], out_sem.at[h]))
+            saves[-1].start()
     for cp in pending:
         cp.wait_send()
+    for cp in saves:
+        cp.wait()
 
 
 def finish(found, terms, code_sums, code_counts, latents, new_sums, new_counts, new_codebook):
@@ -412,20 +471,31 @@
     clips, _, places, width = video.shape
     rows = code_sums.shape[0]
     share, blocks, mates = places // n, n // 4, 4
-    parts = max(1, rows // 64)
+    sizes = [32, 32] + [64] * (rows // 64 - 1)
+    spans = [(sum(sizes[:i]), z) for i, z in enumerate(sizes)]
+    parts = len(spans)
     pieces = 1
     tokens = mates * places
     vmem = pl.BlockSpec(memory_space=pltpu.VMEM)
+    hbm = pl.BlockSpec(memory_space=pl.ANY)
     dma = pltpu.SemaphoreType.DMA
     found, terms = pl.pallas_call(
-        functools.partial(body, n, parts),
+        functools.partial(body, n, spans),
         out_shape=(
             jax.ShapeDtypeStruct((clips, n, share, width), F32),
             jax.ShapeDtypeStruct((rows + 8, width), F32),
         ),
-        in_specs=[vmem, pl.BlockSpec(memory_space=pltpu.SMEM)] + [vmem] * 8,
-        out_specs=(vmem,) * 2,
+        in_specs=[hbm, pl.BlockSpec(memory_space=pltpu.SMEM), vmem, hbm, hbm, vmem, hbm, hbm, hbm, vmem],
+        out_specs=(hbm,) * 2,
         scratch_shapes=[
+            pltpu.VMEM((clips, places, width), F32),
+            pltpu.VMEM((width, 3 * width), F32),
+            pltpu.VMEM((width, width), F32),
+            pltpu.VMEM((width, 3 * width), F32),
+            pltpu.VMEM((width, width), F32),
+            pltpu.VMEM((rows, width), F32),
+            pltpu.VMEM((clips, n, share, width), F32),
+            dma((7,)), dma((clips,)), dma((parts,)),
             pltpu.VMEM((clips, places, width), F32),
             pltpu.VMEM((clips, pieces, n, share // pieces, width), F32),
             pltpu.VMEM((blocks, rows, width), F32),

time: 69.4 us -> 66.4 us (0.957)
  Pallas kernels: 68.6 us -> 65.6 us
    pallas_call x1, Pallas kernels: 66.4 us -> 63.4 us  [local(): pl.pallas_call(functools.partial(body, n, spans), out_shape=(jax.ShapeDty...]
where the time goes in v2:
time: 66.4 us; the launch traced here: 66.2 us
  Pallas kernels  65.6 us (99%)
    pallas_call x1, Pallas kernels, local(): pl.pallas_call(functools.partial(body, n, spans), out_shape=(jax.ShapeDty...  63.4 us
    pallas_call x1, Pallas kernels, local(): pl.pallas_call(finish, out_shape=(jax.ShapeDtypeStruct((clips, n, share,...  2.21 us

profile of v2, /device:TPU:0, one launch (start us, length us, event | category | flops | bytes accessed | tf_op | source)
XLA Modules:
  0.0 66.2 jit_solution(14502256818641022548)
XLA Ops:
  0.6 63.4 %tokenizer.1 = (f32[2,16,16,256]{3,2,1,0:T(8,128)}, f32[264,256]{1,0:T(8,128)}) custom-call(f32[2,256,256]{2,1,0:T(8,128)} %bitcast.5, s32[2]{0:T(128)} %starts.1, f32[1,256]{1,0:T(1,128)} %bitcast.8, f32[256,768]{1,0:T(8,128)} %qkv_space_in.1, f32[256,256]{1,0:T(8,128)} %out_space_in.1, f32[1,256]{1,0:T(1,128)} %bitcast.9, f32[256,768]{1,0:T(8,128)} %qkv_time_in.1, ...), custom_call_target="tpu_custom_call" | custom-call | tf_op jit(solution)/shard_map/tokenizer/pallas_call | solution.py:482
  64.0 2.2 %finish.1 = (f32[2,16,16,256]{3,2,1,0:T(8,128)}, f32[256,256]{1,0:T(8,128)}, f32[1,256]{1,0:T(1,128)}, f32[256,256]{1,0:T(8,128)}) custom-call(f32[2,16,16,256]{3,2,1,0:T(8,128)} %get-tuple-element.10.found, f32[264,256]{1,0:T(8,128)} %get-tuple-element.11.terms, f32[256,256]{1,0:T(8,128)} %code_sums.1, f32[1,256]{1,0:T(1,128)} %bitcast.7), custom_call_target="tpu_custom_call" | custom-call | tf_op jit(solution)/shard_map/finish/pallas_call | solution.py:525

commit v3 on v2

--- a/solution.py
+++ b/solution.py
@@ -227,7 +227,7 @@
     def await_tokens(c, h, q):
         token_copy(c, h, q, q, me).wait_recv()
 
-    code_at = [-2, -2, 0, 0]
+    code_at = [-1, -1, 0, 0]
     early = [ch for ch in range(4) if code_at[ch] < 0]
     late = [ch for ch in range(4) if code_at[ch] >= 0]
 
@@ -250,6 +250,8 @@
     loads["out_space"].wait()
     w_q, w_o = split(qkv_space[...]), split(out_space[...])
     gain = gain_space[...]
+    hops = sorted(range(1, n), key=lambda d: abs(2 * d - n))
+
     def deal(c, h, d):
         to = lax.rem(me + d, n)
         send(
@@ -272,7 +274,7 @@
             loads["video%d" % c].wait()
         spaced[c] = attention(video[c], gain, w_q, w_o, None, enter if c == 0 else None)
         if c < 1:
-            for d in range(1, n):
+            for d in hops:
                 deal(*units[c], d)
         keep(c)
     across(-1)
@@ -326,7 +328,7 @@
 
     saves = []
     for i, (c, h) in enumerate(units):
-        for d in range(1, n):
+        for d in hops:
             await_deal(c, h, d)
             if i + 1 < len(units):
                 deal(*units[i + 1], d)

time: 66.4 us -> 65.2 us (0.982)
  Pallas kernels: 65.6 us -> 64.4 us
    pallas_call x1, Pallas kernels: 63.4 us -> 62.1 us  [local(): pl.pallas_call(functools.partial(body, n, spans), out_shape=(jax.ShapeDty...]
where the time goes in v3:
time: 65.2 us; the launch traced here: 65 us
  Pallas kernels  64.4 us (99%)
    pallas_call x1, Pallas kernels, local(): pl.pallas_call(functools.partial(body, n, spans), out_shape=(jax.ShapeDty...  62.1 us
    pallas_call x1, Pallas kernels, local(): pl.pallas_call(finish, out_shape=(jax.ShapeDtypeStruct((clips, n, share,...  2.21 us

profile of v3, /device:TPU:0, one launch (start us, length us, event | category | flops | bytes accessed | tf_op | source)
XLA Modules:
  0.0 65.0 jit_solution(11490830563052770353)
XLA Ops:
  0.6 62.1 %tokenizer.1 = (f32[2,16,16,256]{3,2,1,0:T(8,128)}, f32[264,256]{1,0:T(8,128)}) custom-call(f32[2,256,256]{2,1,0:T(8,128)} %bitcast.5, s32[2]{0:T(128)} %starts.1, f32[1,256]{1,0:T(1,128)} %bitcast.8, f32[256,768]{1,0:T(8,128)} %qkv_space_in.1, f32[256,256]{1,0:T(8,128)} %out_space_in.1, f32[1,256]{1,0:T(1,128)} %bitcast.9, f32[256,768]{1,0:T(8,128)} %qkv_time_in.1, ...), custom_call_target="tpu_custom_call" | custom-call | tf_op jit(solution)/shard_map/tokenizer/pallas_call | solution.py:484
  62.8 2.2 %finish.1 = (f32[2,16,16,256]{3,2,1,0:T(8,128)}, f32[256,256]{1,0:T(8,128)}, f32[1,256]{1,0:T(1,128)}, f32[256,256]{1,0:T(8,128)}) custom-call(f32[2,16,16,256]{3,2,1,0:T(8,128)} %get-tuple-element.10.found, f32[264,256]{1,0:T(8,128)} %get-tuple-element.11.terms, f32[256,256]{1,0:T(8,128)} %code_sums.1, f32[1,256]{1,0:T(1,128)} %bitcast.7), custom_call_target="tpu_custom_call" | custom-call | tf_op jit(solution)/shard_map/finish/pallas_call | solution.py:527

commit v4 on v3

--- a/solution.py
+++ b/solution.py
@@ -281,8 +281,8 @@
     loads["qkv_time"].wait()
     loads["out_time"].wait()
 
-    def ready(c, h):
-        for q in (2 * h, 2 * h + 1):
+    def ready(c, h, quarters=(0, 1)):
+        for q in (2 * h + i for i in quarters):
             if q % 2:
                 for i in range(pieces):
                     await_tokens(c, i, q)
@@ -291,11 +291,12 @@
             unit[at, :] = u.astype(BF16)
             warm[0, at, :], warm[1, at, :] = split(u * (1.0 / SOFTMAX_WARMTH))
 
-    def score(c, h, r):
-        two = 2 * places
-        at = pl.ds(c * tokens + h * two, two)
+    def score(c, h, r, quarter=None):
+        two = 2 * places if quarter is None else places
+        begin = 2 * h * places + (quarter or 0) * places
+        at = pl.ds(c * tokens + begin, two)
         e = jnp.exp(dot3(split(codes[r]), (warm[0, at, :], warm[1, at, :]), NT))
-        at = pl.ds(h * two, two)
+        at = pl.ds(begin, two)
         weights[c, r, :, at] = e
         t = jnp.sum(e.reshape(rows // 8, 8, two), 0)
         total[c, :, at] = t if r == 0 else total[c, :, at] + t
@@ -376,9 +377,10 @@
     share_totals(0)
     for r in odds:
         score(1, 0, r)
-    ready(1, 1)
-    for r in range(blocks):
-        score(1, 1, r)
+    for quarter in range(2):
+        ready(1, 1, (quarter,))
+        for r in range(blocks):
+            score(1, 1, r, quarter)
     share_totals(1)
     ones = jnp.ones((8, lanes), BF16)
 

time: 65.2 us -> 65.2 us (level)
  no operation moved by 1% of the time
where the time goes in v4:
time: 65.2 us; the launch traced here: 65 us
  Pallas kernels  64.4 us (99%)
    pallas_call x1, Pallas kernels, local(): pl.pallas_call(functools.partial(body, n, spans), out_shape=(jax.ShapeDty...  62.2 us
    pallas_call x1, Pallas kernels, local(): pl.pallas_call(finish, out_shape=(jax.ShapeDtypeStruct((clips, n, share,...  2.21 us

profile of v4, /device:TPU:0, one launch (start us, length us, event | category | flops | bytes accessed | tf_op | source)
XLA Modules:
  0.0 65.0 jit_solution(5763093137606067717)
XLA Ops:
  0.6 62.2 %tokenizer.1 = (f32[2,16,16,256]{3,2,1,0:T(8,128)}, f32[264,256]{1,0:T(8,128)}) custom-call(f32[2,256,256]{2,1,0:T(8,128)} %bitcast.5, s32[2]{0:T(128)} %starts.1, f32[1,256]{1,0:T(1,128)} %bitcast.8, f32[256,768]{1,0:T(8,128)} %qkv_space_in.1, f32[256,256]{1,0:T(8,128)} %out_space_in.1, f32[1,256]{1,0:T(1,128)} %bitcast.9, f32[256,768]{1,0:T(8,128)} %qkv_time_in.1, ...), custom_call_target="tpu_custom_call" | custom-call | tf_op jit(solution)/shard_map/tokenizer/pallas_call | solution.py:486
  62.8 2.2 %finish.1 = (f32[2,16,16,256]{3,2,1,0:T(8,128)}, f32[256,256]{1,0:T(8,128)}, f32[1,256]{1,0:T(1,128)}, f32[256,256]{1,0:T(8,128)}) custom-call(f32[2,16,16,256]{3,2,1,0:T(8,128)} %get-tuple-element.10.found, f32[264,256]{1,0:T(8,128)} %get-tuple-element.11.terms, f32[256,256]{1,0:T(8,128)} %code_sums.1, f32[1,256]{1,0:T(1,128)} %bitcast.7), custom_call_target="tpu_custom_call" | custom-call | tf_op jit(solution)/shard_map/finish/pallas_call | solution.py:529
